TPU v7x, 32 devices: a whole 2x2x4 slice. The times are simulated.
32 devices in a mesh: fsdp: 4 (over x, core), ctx: 4 (over z), tp: 2 (over y).
Axes of the slice: x: 2, y: 2, z: 4, core: 2. Of those that a mesh axis runs over, the one named last changes fastest.
Arguments:
- tokens: bfloat16 [8, 4096, 768], P('fsdp', 'ctx'), may hold values from -6 to 6
- qkv_weight: bfloat16 [768, 3, 768], P(('fsdp', 'ctx'), None, 'tp'), may hold values from -0.21875 to 0.21875
- qv_bias: bfloat16 [2, 768], P(None, 'tp'), may hold values from -3 to 3
- out_weight: bfloat16 [768, 768], P(('fsdp', 'ctx'), 'tp'), may hold values from -8 to 8
- up_weight: bfloat16 [768, 3072], P(('fsdp', 'ctx'), 'tp'), may hold values from -0.21875 to 0.21875
- up_bias: bfloat16 [3072], P('tp'), may hold values from -3 to 3
- down_weight: bfloat16 [768, 3072], P(('fsdp', 'ctx'), 'tp'), may hold values from -0.109375 to 0.109375
- norm_gains: bfloat16 [768, 2], P(('fsdp', 'ctx')), may hold values from 0.5 to 1.5
- row_biases: bfloat16 [768, 4], P(('fsdp', 'ctx')), may hold values from -3 to 3
- cotangent: bfloat16 [8, 4096, 768], P('fsdp', 'ctx'), may hold values from -6 to 6
Outputs:
- output: bfloat16 [8, 4096, 768], P('fsdp', ('ctx', 'tp'))
- tokens_grad: bfloat16 [8, 4096, 768], P('fsdp', ('ctx', 'tp'))
- qkv_weight_grad: float32 [768, 3, 768], P(('fsdp', 'ctx'), None, 'tp')
- qv_bias_grad: float32 [2, 768], P(None, 'tp')
- out_weight_grad: float32 [768, 768], P(('fsdp', 'ctx'), 'tp')
- up_weight_grad: float32 [768, 3072], P(('fsdp', 'ctx'), 'tp')
- up_bias_grad: float32 [3072], P('tp')
- down_weight_grad: float32 [768, 3072], P(('fsdp', 'ctx'), 'tp')
- norm_gains_grad: float32 [768, 2], P(('fsdp', 'ctx'))
- row_biases_grad: float32 [768, 4], P(('fsdp', 'ctx'))
All inputs are finite; a program needn't handle non-finite values.
Results may differ from a plain program's by a relative error of at most 0.02.
Values may be sent and summed in bfloat16 or wider, within the bound.
No kernel may reach another device: no remote copies, remote signals or barrier semaphores. Data moves between devices by JAX's collectives and lax.ppermute only.
A program may use at most 256 MiB of HBM per device.

v0:
```python
import jax
import jax.numpy as jnp
from jax import lax
from jax.sharding import PartitionSpec as P

HD = 64
epsilon = 1e-12
score_scale = 0.125
highest = lax.Precision.HIGHEST


def contract_last(left, right):
    return lax.dot_general(
        left, right, (((1,), (1,)), ((), ())), preferred_element_type=jnp.float32
    )


def contract_first(left, right):
    return lax.dot_general(
        left, right, (((0,), (0,)), ((), ())), preferred_element_type=jnp.float32
    )


def norm_forward(hidden, gain, shift):
    center = hidden - jnp.mean(hidden, axis=-1, keepdims=True)
    inv_scale = lax.rsqrt(jnp.mean(center * center, axis=-1, keepdims=True) + epsilon)
    normed = center * inv_scale
    return (normed * gain + shift, normed, inv_scale)


def norm_backward(grad_out, normed, inv_scale, gain):
    grad_norm = grad_out * gain
    return inv_scale * (
        grad_norm
        - jnp.mean(grad_norm, axis=-1, keepdims=True)
        - normed * jnp.mean(grad_norm * normed, axis=-1, keepdims=True)
    )


def gelu_exact(values):
    return jax.nn.gelu(values, approximate=False)


def split_heads(array, first_row, row_count, head_count):
    piece = lax.dynamic_slice_in_dim(array, first_row, row_count, 1)
    return piece.reshape(piece.shape[0], row_count, head_count, piece.shape[2] // head_count)


def block_scores(query_four, key_four):
    return (
        jnp.einsum("sqhd,skhd->shqk", query_four, key_four, preferred_element_type=jnp.float32)
        * score_scale
    )


def softmax_rows(scores, row_max, row_total):
    return jnp.exp(scores - row_max[..., None]) / row_total[..., None]


def score_grads(scores, row_max, row_total, row_delta, grad_four, value_four):
    prob_full = softmax_rows(scores, row_max, row_total)
    prob_grad = jnp.einsum(
        "sqhd,skhd->shqk", grad_four, value_four, preferred_element_type=jnp.float32
    )
    score_low = (prob_full * (prob_grad - row_delta[..., None])).astype(jnp.bfloat16)
    return (prob_full.astype(jnp.bfloat16), score_low)


def body(
    tokens,
    qkv_weight,
    qv_bias,
    out_weight,
    up_weight,
    up_bias,
    down_weight,
    norm_gains,
    row_biases,
    cotangent,
):
    seq_count, local_len, width = tokens.shape
    row_count = seq_count * local_len
    tp_count = lax.axis_size("tp")
    share_len = local_len // tp_count
    share_start = lax.axis_index("tp") * share_len

    def own_rows(array_three):
        return lax.dynamic_slice_in_dim(array_three, share_start, share_len, 1)

    def to_three(array_two):
        return array_two.reshape(seq_count, array_two.shape[0] // seq_count, array_two.shape[1])

    gathered = (
        lax.all_gather(qkv_weight, ("fsdp", "ctx"), axis=0, tiled=True),
        lax.all_gather(out_weight, ("fsdp", "ctx"), axis=0, tiled=True),
        lax.all_gather(up_weight, ("fsdp", "ctx"), axis=0, tiled=True),
        lax.all_gather(down_weight, ("fsdp", "ctx"), axis=0, tiled=True),
        lax.all_gather(norm_gains, ("fsdp", "ctx"), axis=0, tiled=True),
        lax.all_gather(row_biases, ("fsdp", "ctx"), axis=0, tiled=True),
    )
    w_qkv, w_out, w_up, w_down, gains_all, biases_all = gathered
    gains_f = gains_all.astype(jnp.float32)
    biases_f = biases_all.astype(jnp.float32)
    head_width = w_qkv.shape[2]
    head_count = head_width // HD
    flat_tokens = tokens.reshape(row_count, width)
    projected = jnp.dot(
        flat_tokens, w_qkv.reshape(width, 3 * head_width), preferred_element_type=jnp.float32
    )
    projected = projected.reshape(row_count, 3, head_width)
    bias_f = qv_bias.astype(jnp.float32)
    query_low = (projected[:, 0] + bias_f[0]).astype(jnp.bfloat16)
    key_low = projected[:, 1].astype(jnp.bfloat16)
    value_low = (projected[:, 2] + bias_f[1]).astype(jnp.bfloat16)
    keys_full, values_full = (
        lax.all_gather(
            key_low.reshape(seq_count, local_len, head_width), "ctx", axis=1, tiled=True
        ),
        lax.all_gather(
            value_low.reshape(seq_count, local_len, head_width), "ctx", axis=1, tiled=True
        ),
    )
    full_len = keys_full.shape[1]
    block_len = min(512, full_len)
    block_count = full_len // block_len
    query_four = query_low.reshape(seq_count, local_len, head_count, HD)
    stat_shape = (seq_count, head_count, local_len)
    four_shape = (seq_count, local_len, head_count, HD)

    def stats_step(block_idx, running):
        row_max, row_total = running
        scores = block_scores(
            query_four, split_heads(keys_full, block_idx * block_len, block_len, head_count)
        )
        new_max = jnp.maximum(row_max, jnp.max(scores, axis=-1))
        row_total = row_total * jnp.exp(row_max - new_max) + jnp.sum(
            jnp.exp(scores - new_max[..., None]), axis=-1
        )
        return (new_max, row_total)

    row_max, row_total = lax.fori_loop(
        0,
        block_count,
        stats_step,
        (jnp.full(stat_shape, -jnp.inf, jnp.float32), jnp.zeros(stat_shape, jnp.float32)),
    )

    def value_step(block_idx, attn_mixed):
        first_row = block_idx * block_len
        value_four = split_heads(values_full, first_row, block_len, head_count)
        prob_full = softmax_rows(
            block_scores(query_four, split_heads(keys_full, first_row, block_len, head_count)),
            row_max,
            row_total,
        )
        return attn_mixed + jnp.einsum(
            "shqk,skhd->sqhd",
            prob_full.astype(jnp.bfloat16),
            value_four,
            preferred_element_type=jnp.float32,
        )

    zero_four = jnp.zeros(four_shape, jnp.float32)
    attn_mixed = lax.fori_loop(0, block_count, value_step, zero_four)
    mixed_low = attn_mixed.reshape(row_count, head_width).astype(jnp.bfloat16)
    attn_part = contract_last(mixed_low, w_out)
    attn_out = lax.psum(attn_part.astype(jnp.bfloat16), "tp").astype(jnp.float32) + biases_f[:, 0]
    first_out, first_norm, first_scale = norm_forward(
        flat_tokens.astype(jnp.float32) + attn_out, gains_f[:, 0], biases_f[:, 1]
    )
    first_low = first_out.astype(jnp.bfloat16)
    inner_pre = jnp.dot(first_low, w_up, preferred_element_type=jnp.float32) + up_bias.astype(
        jnp.float32
    )
    activated, gelu_back = jax.vjp(gelu_exact, inner_pre)
    act_low = activated.astype(jnp.bfloat16)
    ffn_part = contract_last(act_low, w_down)
    ffn_out = lax.psum(ffn_part.astype(jnp.bfloat16), "tp").astype(jnp.float32) + biases_f[:, 2]
    grad_final = cotangent.reshape(row_count, width).astype(jnp.float32)
    final_out, final_norm, final_scale = norm_forward(
        first_out + ffn_out, gains_f[:, 1], biases_f[:, 3]
    )
    gain2_grad = jnp.sum(grad_final * final_norm, axis=0)
    shift2_grad = jnp.sum(grad_final, axis=0)
    grad_second = norm_backward(grad_final, final_norm, final_scale, gains_f[:, 1])
    ffn_grad_low = grad_second.astype(jnp.bfloat16)
    down_grad = contract_first(ffn_grad_low, act_low)
    down_bias_grad = jnp.sum(ffn_grad_low.astype(jnp.float32), axis=0)
    act_grad = jnp.dot(ffn_grad_low, w_down, preferred_element_type=jnp.float32)
    inner_low = gelu_back(act_grad)[0].astype(jnp.bfloat16)
    up_grad = contract_first(first_low, inner_low)
    up_bias_grad = jnp.sum(inner_low.astype(jnp.float32), axis=0)
    back_part = contract_last(inner_low, w_up)
    first_grad = grad_second + lax.psum(back_part.astype(jnp.bfloat16), "tp").astype(jnp.float32)
    gain1_grad = jnp.sum(first_grad * first_norm, axis=0)
    shift1_grad = jnp.sum(first_grad, axis=0)
    resid_grad = norm_backward(first_grad, first_norm, first_scale, gains_f[:, 0])
    attn_grad_low = resid_grad.astype(jnp.bfloat16)
    out_grad = contract_first(attn_grad_low, mixed_low)
    out_bias_grad = jnp.sum(attn_grad_low.astype(jnp.float32), axis=0)
    mixed_grad_low = jnp.dot(attn_grad_low, w_out, preferred_element_type=jnp.float32).astype(
        jnp.bfloat16
    )
    grad_four = mixed_grad_low.reshape(four_shape)
    row_delta = jnp.einsum(
        "sqhd,sqhd->shq", grad_four.astype(jnp.float32), attn_mixed, precision=highest
    )

    def grad_step(block_idx, running):
        query_grad, key_all, value_all = running
        first_row = block_idx * block_len
        key_four = split_heads(keys_full, first_row, block_len, head_count)
        value_four = split_heads(values_full, first_row, block_len, head_count)
        scores = block_scores(query_four, key_four)
        prob_low, score_low = score_grads(
            scores, row_max, row_total, row_delta, grad_four, value_four
        )
        query_grad = query_grad + jnp.einsum(
            "shqk,skhd->sqhd", score_low, key_four, preferred_element_type=jnp.float32
        )
        key_part = (
            jnp.einsum("shqk,sqhd->skhd", score_low, query_four, preferred_element_type=jnp.float32)
            * score_scale
        )
        value_part = jnp.einsum(
            "shqk,sqhd->skhd", prob_low, grad_four, preferred_element_type=jnp.float32
        )
        key_all = lax.dynamic_update_slice_in_dim(
            key_all, key_part.reshape(seq_count, block_len, head_width), first_row, 1
        )
        value_all = lax.dynamic_update_slice_in_dim(
            value_all, value_part.reshape(seq_count, block_len, head_width), first_row, 1
        )
        return (query_grad, key_all, value_all)

    zeros_full = jnp.zeros((seq_count, full_len, head_width), jnp.float32)
    query_grad, key_all, value_all = lax.fori_loop(
        0, block_count, grad_step, (zero_four, zeros_full, zeros_full)
    )
    key_grad, value_grad = (
        lax.psum_scatter(
            key_all.astype(jnp.bfloat16), "ctx", scatter_dimension=1, tiled=True
        ).astype(jnp.float32),
        lax.psum_scatter(
            value_all.astype(jnp.bfloat16), "ctx", scatter_dimension=1, tiled=True
        ).astype(jnp.float32),
    )
    query_grad_low = (query_grad * score_scale).reshape(row_count, head_width).astype(jnp.bfloat16)
    key_grad_low = key_grad.reshape(row_count, head_width).astype(jnp.bfloat16)
    value_grad_low = value_grad.reshape(row_count, head_width).astype(jnp.bfloat16)
    grad_cat = jnp.stack([query_grad_low, key_grad_low, value_grad_low], axis=1)
    qkv_grad = jnp.einsum("td,tcj->dcj", flat_tokens, grad_cat, preferred_element_type=jnp.float32)
    qv_grad = jnp.stack(
        [
            jnp.sum(query_grad_low.astype(jnp.float32), axis=0),
            jnp.sum(value_grad_low.astype(jnp.float32), axis=0),
        ]
    )
    input_part = contract_last(
        grad_cat.reshape(row_count, 3 * head_width), w_qkv.reshape(width, 3 * head_width)
    )
    gains_grad = jnp.stack([gain1_grad, gain2_grad], axis=1)
    shifts_grad = jnp.stack([shift1_grad, shift2_grad], axis=1)
    tokens_full = resid_grad + lax.psum(input_part.astype(jnp.bfloat16), "tp").astype(jnp.float32)
    tokens_share = own_rows(to_three(tokens_full))
    output_share = own_rows(to_three(final_out))
    biases_grad = jnp.stack(
        [out_bias_grad, shifts_grad[:, 0], down_bias_grad, shifts_grad[:, 1]], axis=1
    )
    shards = (
        lax.psum_scatter(qkv_grad, ("fsdp", "ctx"), scatter_dimension=0, tiled=True),
        lax.psum_scatter(out_grad, ("fsdp", "ctx"), scatter_dimension=0, tiled=True),
        lax.psum_scatter(up_grad, ("fsdp", "ctx"), scatter_dimension=0, tiled=True),
        lax.psum_scatter(down_grad, ("fsdp", "ctx"), scatter_dimension=0, tiled=True),
        lax.psum_scatter(gains_grad, ("fsdp", "ctx"), scatter_dimension=0, tiled=True),
        lax.psum_scatter(biases_grad, ("fsdp", "ctx"), scatter_dimension=0, tiled=True),
    )
    qv_total, up_total = lax.psum((qv_grad, up_bias_grad), ("fsdp", "ctx"))
    output = output_share.astype(jnp.bfloat16)
    tokens_out = tokens_share.astype(jnp.bfloat16)
    return (
        output,
        tokens_out,
        shards[0],
        qv_total,
        shards[1],
        shards[2],
        up_total,
        shards[3],
        shards[4],
        shards[5],
    )


def solution(mesh):
    in_specs = (
        P("fsdp", "ctx", None),
        P(("fsdp", "ctx"), None, "tp"),
        P(None, "tp"),
        P(("fsdp", "ctx"), "tp"),
        P(("fsdp", "ctx"), "tp"),
        P("tp"),
        P(("fsdp", "ctx"), "tp"),
        P(("fsdp", "ctx"), None),
        P(("fsdp", "ctx"), None),
        P("fsdp", "ctx", None),
    )
    out_specs = (
        P("fsdp", ("ctx", "tp"), None),
        P("fsdp", ("ctx", "tp"), None),
        P(("fsdp", "ctx"), None, "tp"),
        P(None, "tp"),
        P(("fsdp", "ctx"), "tp"),
        P(("fsdp", "ctx"), "tp"),
        P("tp"),
        P(("fsdp", "ctx"), "tp"),
        P(("fsdp", "ctx"), None),
        P(("fsdp", "ctx"), None),
    )
    return jax.shard_map(body, mesh=mesh, in_specs=in_specs, out_specs=out_specs, check_vma=False)
```

profile of v0, /device:TPU:0, one launch (start us, length us, event | category | flops | bytes accessed | tf_op | source)
XLA Modules:
  0.0 2090.9 jit_solution(9542823779875088038)
XLA Ops:
  8.0 45.5 %all-gather.8.cloned.1.call-done = bf16[768,3,384]{2,0,1:T(8,128)(2,1)} async-done(((bf16[48,3,384]{2,0,1:T(8,128)(2,1)}), bf16[768,3,384]{2,0,1:T(8,128)(2,1)}) %all-gather.8.cloned.1.call-update) | async-done | bytes 1769488 | tf_op jit(solution)/shard_map/all_gather | solution.py:94
  67.9 53.4 %all_gather.27 = bf16[768,384]{1,0:T(8,128)(2,1)} all-gather(bf16[48,384]{1,0:T(8,128)(2,1)S(1)} %copy-done.33), channel_id=1, replica_groups=mesh['fsdp'=4,'ctx'=4,'tp'=2] {'fsdp','ctx'}, dimensions={0}, use_global_device_ids=true | all-gather | bytes 626688 | tf_op jit(solution)/shard_map/all_gather | solution.py:95
  142.1 48.3 %all-gather.12.cloned.1.call-done = bf16[2,4096,384]{1,2,0:T(8,128)(2,1)} async-done(((bf16[2,1024,384]{1,2,0:T(8,128)(2,1)}), bf16[2,4096,384]{1,2,0:T(8,128)(2,1)}) %all-gather.12.cloned.1.call-update) | async-done | bytes 6291472 | tf_op jit(solution)/shard_map/all_gather | solution.py:116
  190.4 93.1 %while.48 = (s32[]{:T(128)}, f32[2,6,1024]{2,1,0:T(8,128)S(1)}, f32[2,6,1024]{2,1,0:T(8,128)S(1)}, bf16[2,4096,384]{1,2,0:T(8,128)(2,1)}, bf16[2,1024,6,64]{1,3,...) while((s32[]{:T(128)}, f32[2,6,1024]{2,1,0:T(8,128)S(1)}, ...), condition=%wide.region_3.0_spmd.clone, body=%wide.region_0.0_spmd.clone.sunk | while | flops 836825088 | bytes 54902944 | solution.py:141
  283.4 22.7 %all-gather.10.cloned.1.call-done = bf16[2,4096,384]{1,2,0:T(8,128)(2,1)} async-done(((bf16[2,1024,384]{1,2,0:T(8,128)(2,1)}), bf16[2,4096,384]{1,2,0:T(8,128)(2,1)}) %all-gather.10.cloned.1.call-update) | async-done | bytes 6291472 | tf_op jit(solution)/shard_map/all_gather | solution.py:119
  306.2 88.7 %while.49 = (s32[]{:T(128)}, f32[2,1024,6,64]{1,3,2,0:T(8,128)}, bf16[2,4096,384]{1,2,0:T(8,128)(2,1)}, bf16[2,4096,384]{1,2,0:T(8,128)(2,1)}, bf16[2,1024,6,64]...) while((s32[]{:T(128)}, f32[2,1024,6,64]{1,3,2,0:T(8,128)}, ...), condition=%wide.region_5.0_spmd.clone, body=%wide.region_4.0_spmd.clone.sunk | while | flops 1637351424 | bytes 12681393 | solution.py:164
  318.3 9.7 bitcast_add_fusion.4
  329.5 9.7 bitcast_add_fusion.4
  340.6 9.7 bitcast_add_fusion.4
  351.8 9.7 bitcast_add_fusion.4
  362.9 9.7 bitcast_add_fusion.4
  374.1 9.7 bitcast_add_fusion.4
  385.2 9.7 bitcast_add_fusion.4
  405.1 29.4 %all-gather.1 = bf16[16,48,2]{1,2,0:T(2,128)(2,1)S(1)} all-gather(bf16[1,48,2]{1,2,0:T(2,128)(2,1)S(1)} %bitcast.191), channel_id=1, replica_groups=mesh['fsdp'=4,'ctx'=4,'tp'=2] {'fsdp','ctx'}, dimensions={0}, use_global_device_ids=true | all-gather | bytes 3264 | tf_op jit(solution)/shard_map/all_gather | solution.py:98
  434.7 29.8 %all-gather = bf16[16,48,4]{1,2,0:T(4,128)(2,1)S(1)} all-gather(bf16[1,48,4]{1,2,0:T(4,128)(2,1)S(1)} %bitcast.190), channel_id=1, replica_groups=mesh['fsdp'=4,'ctx'=4,'tp'=2] {'fsdp','ctx'}, dimensions={0}, use_global_device_ids=true | all-gather | bytes 6528 | tf_op jit(solution)/shard_map/all_gather | solution.py:99
  465.2 22.8 %all-reduce.8.cloned.1.call-done = bf16[2048,768]{1,0:T(8,128)(2,1)} async-done(((bf16[2048,768]{1,0:T(8,128)(2,1)}), bf16[2048,768]{1,0:T(8,128)(2,1)}) %all-reduce.8.cloned.1.call-update) | async-done | bytes 3145744 | tf_op jit(solution)/shard_map/psum | solution.py:167
  496.9 35.6 %all-gather.14.cloned.1.call-done = bf16[768,1536]{1,0:T(8,128)(2,1)} async-done(((bf16[48,1536]{1,0:T(8,128)(2,1)}), bf16[768,1536]{1,0:T(8,128)(2,1)}) %all-gather.14.cloned.1.call-update) | async-done | bytes 2359312 | tf_op jit(solution)/shard_map/all_gather | solution.py:96
  532.5 35.1 %multiply_convert_fusion.1 = (bf16[2048,1536]{1,0:T(8,128)(2,1)}, f32[2048,1536]{1,0:T(8,128)}, f32[2048,1536]{1,0:T(8,128)}) fusion(f32[1536]{0:T(1024)S(1)} %convert_element_type.186, bf16[768,1536]{1,0:T(8,128)(2,1)} %all-gather.14.cloned.1.call-done, f32[2048,768]{1,0:T(8,128)} %subtract_multiply_fusion.2, f32[768]{0:T(1024)S(1)} %get-tuple-element.637, ...), kind=kOutput, calls=%fused_computation.29 | convolution fusion | flops 5044174848 | bytes 40120320 | tf_op jit(solution)/shard_map/dot_general | solution.py:172
  587.0 82.7 %all-reduce.10.cloned.1.call-done = bf16[2048,768]{1,0:T(8,128)(2,1)} async-done(((bf16[2048,768]{1,0:T(8,128)(2,1)}), bf16[2048,768]{1,0:T(8,128)(2,1)}) %all-reduce.10.cloned.1.call-update) | async-done | bytes 3145744 | tf_op jit(solution)/shard_map/psum | solution.py:178
  681.4 18.9 convert_reduce_fusion
  709.4 85.9 %all-reduce.12.cloned.1.call-done = bf16[2048,768]{1,0:T(8,128)(2,1)} async-done(((bf16[2048,768]{1,0:T(8,128)(2,1)}), bf16[2048,768]{1,0:T(8,128)(2,1)}) %all-reduce.12.cloned.1.call-update) | async-done | bytes 3145744 | tf_op jit(solution)/shard_map/psum | solution.py:194
  795.3 9.7 multiply_reduce_fusion
  830.2 482.1 %while.50 = (s32[]{:T(128)}, f32[2,1024,6,64]{1,3,2,0:T(8,128)}, bf16[2,4096,384]{1,2,0:T(8,128)(2,1)}, bf16[2,4096,384]{1,2,0:T(8,128)(2,1)}, bf16[2,4096,384]{...) while((s32[]{:T(128)}, f32[2,1024,6,64]{1,3,2,0:T(8,128)}, ...), condition=%wide.region_18.0_spmd.clone, body=%wide.region_17.0_spmd.clone.sunk | while | flops 4072931328 | bytes 139346160 | solution.py:237
  832.8 12.5 exponential_divide_fusion.2
  845.3 11.2 fusion.106
  856.5 14.5 multiply_convert_fusion.5
  892.2 12.5 exponential_divide_fusion.2
  904.7 11.2 fusion.106
  915.8 14.5 multiply_convert_fusion.5
  939.3 9.5 bitcast_add_fusion.5
  952.5 12.5 exponential_divide_fusion.2
  965.0 11.2 fusion.106
  976.1 14.5 multiply_convert_fusion.5
  999.6 9.5 bitcast_add_fusion.5
  1012.8 12.5 exponential_divide_fusion.2
  1025.3 11.2 fusion.106
  1036.4 14.5 multiply_convert_fusion.5
  1059.9 9.5 bitcast_add_fusion.5
  1073.1 12.5 exponential_divide_fusion.2
  1085.6 11.2 fusion.106
  1096.7 14.5 multiply_convert_fusion.5
  1120.2 9.5 bitcast_add_fusion.5
  1133.4 12.5 exponential_divide_fusion.2
  1145.9 11.2 fusion.106
  1157.1 14.5 multiply_convert_fusion.5
  1180.5 9.5 bitcast_add_fusion.5
  1193.9 12.5 exponential_divide_fusion.2
  1206.4 11.2 fusion.106
  1217.5 14.5 multiply_convert_fusion.5
  1241.0 9.5 bitcast_add_fusion.5
  1254.3 12.5 exponential_divide_fusion.2
  1266.8 11.2 fusion.106
  1277.9 14.5 multiply_convert_fusion.5
  1328.0 95.3 %reduce-scatter.12.cloned.1.call-done = bf16[2,1024,384]{1,2,0:T(8,128)(2,1)} async-done(((bf16[2,4096,384]{1,2,0:T(8,128)(2,1)}), bf16[2,1024,384]{1,2,0:T(8,128)(2,1)}) %reduce-scatter.12.cloned.1.call-update) | async-done | bytes 1572880 | tf_op jit(solution)/shard_map/reduce_scatter | solution.py:241
  1425.9 110.9 %reduce-scatter.14.cloned.1.call-done = bf16[2,1024,384]{1,2,0:T(8,128)(2,1)} async-done(((bf16[2,4096,384]{1,2,0:T(8,128)(2,1)}), bf16[2,1024,384]{1,2,0:T(8,128)(2,1)}) %reduce-scatter.14.cloned.1.call-update) | async-done | bytes 1572880 | tf_op jit(solution)/shard_map/reduce_scatter | solution.py:244
  1568.5 10.4 fusion.35
  1579.1 10.5 fusion.26
  1598.2 57.1 %reduce-scatter.24.cloned.1.call-done = f32[48,4]{1,0:T(8,128)} async-done(((f32[768,4]{1,0:T(8,128)}), f32[48,4]{1,0:T(8,128)}) %reduce-scatter.24.cloned.1.call-update) | async-done | bytes 784
  1656.9 61.1 %all-reduce.1 = (f32[2,384]{1,0:T(2,128)}, f32[1536]{0:T(1024)}) all-reduce(f32[2,384]{1,0:T(2,128)S(1)} %pad_maximum_fusion.5, f32[1536]{0:T(1024)S(1)} %copy-done.43), channel_id=1, replica_groups=mesh['fsdp'=4,'ctx'=4,'tp'=2] {'fsdp','ctx'}, use_global_device_ids=true, to_apply=%region_25.0 | all-reduce | flops 2304 | bytes 18432 | tf_op jit(solution)/shard_map/psum | solution.py:278
  1718.1 58.1 %all-reduce.16.cloned.1.call-done = f32[768,3,384]{2,1,0:T(4,128)} async-done(((f32[768,3,384]{2,1,0:T(4,128)}), f32[768,3,384]{2,1,0:T(4,128)}) %all-reduce.16.cloned.1.call-update) | async-done | bytes 3538960
  1777.8 86.1 %all-reduce.14.cloned.1.call-done = bf16[2048,768]{1,0:T(8,128)(2,1)} async-done(((bf16[2048,768]{1,0:T(8,128)(2,1)}), bf16[2048,768]{1,0:T(8,128)(2,1)}) %all-reduce.14.cloned.1.call-update) | async-done | bytes 3145744 | tf_op jit(solution)/shard_map/psum | solution.py:264
  1869.6 56.6 %reduce-scatter.16.cloned.1.call-done = f32[48,384]{1,0:T(8,128)} async-done(((f32[768,384]{1,0:T(8,128)}), f32[48,384]{1,0:T(8,128)}) %reduce-scatter.16.cloned.1.call-update) | async-done | bytes 73744 | tf_op jit(solution)/shard_map/reduce_scatter | solution.py:272
  1926.2 78.9 %reduce-scatter.20.cloned.1.call-done = f32[48,1536]{1,0:T(8,128)} async-done(((f32[768,1536]{1,0:T(8,128)}), f32[48,1536]{1,0:T(8,128)}) %reduce-scatter.20.cloned.1.call-update) | async-done | bytes 294928 | tf_op jit(solution)/shard_map/reduce_scatter | solution.py:274
  2005.0 79.2 %reduce-scatter.18.cloned.1.call-done = f32[48,1536]{1,0:T(8,128)} async-done(((f32[768,1536]{1,0:T(8,128)}), f32[48,1536]{1,0:T(8,128)}) %reduce-scatter.18.cloned.1.call-update) | async-done | bytes 294928 | tf_op jit(solution)/shard_map/reduce_scatter | solution.py:273
  (328 shorter events, 420.7 us)
Async XLA Ops:
  7.2 46.2 %all-gather.8.cloned.1.call-start = ((), (), s32[]{:S(2)}) async-start(), calls=%async_computation.7 | async-start | bytes 1880064 | tf_op jit(solution)/shard_map/all_gather | solution.py:94
  7.9 182.5 %all-gather.12.cloned.1.call-start = ((), (), s32[]{:S(2)}) async-start(), calls=%async_computation.9 | async-start | bytes 7864320 | tf_op jit(solution)/shard_map/all_gather | solution.py:116
  62.2 3.6 copy-start.14
  65.8 2.0 copy-start.33
  67.7 238.5 %all-gather.10.cloned.1.call-start = ((), (), s32[]{:S(2)}) async-start(), calls=%async_computation.8 | async-start | bytes 7864320 | tf_op jit(solution)/shard_map/all_gather | solution.py:119
  141.9 346.1 %all-reduce.8.cloned.1.call-start = ((), (), s32[]{:S(2)}) async-start(), calls=%async_computation.10 | async-start | bytes 6291456 | tf_op jit(solution)/shard_map/psum | solution.py:167
  394.9 8.9 copy-start.12
  394.9 9.0 copy-start.21
  394.9 5.5 copy-start.18
  400.3 4.7 copy-start.44
  400.4 4.7 copy-start.47
  400.4 34.3 %copy-start.46 = (bf16[48,4]{0,1:T(4,128)(2,1)S(1)}, bf16[48,4]{0,1:T(4,128)(2,1)}, u32[]{:S(2)}) copy-start(bf16[48,4]{0,1:T(4,128)(2,1)} %param.24) | copy-start | bytes 1156
  400.4 87.7 %copy-start.7 = (bf16[2,1024,768]{2,1,0:T(8,128)(2,1)S(1)}, bf16[2,1024,768]{2,1,0:T(8,128)(2,1)}, u32[]{:S(2)}) copy-start(bf16[2,1024,768]{2,1,0:T(8,128)(2,1)} %param.16) | copy-start | bytes 9437188
  403.9 128.7 %all-gather.14.cloned.1.call-start = ((), (), s32[]{:S(2)}) async-start(), calls=%async_computation.11 | async-start | bytes 2506752 | tf_op jit(solution)/shard_map/all_gather | solution.py:96
  404.4 171.3 %all-gather.16.cloned.1.call-start = ((), (), s32[]{:S(2)}) async-start(), calls=%async_computation.12 | async-start | bytes 2506752 | tf_op jit(solution)/shard_map/all_gather | solution.py:97
  405.0 264.7 %all-reduce.10.cloned.1.call-start = ((), (), s32[]{:S(2)}) async-start(), calls=%async_computation.13 | async-start | bytes 6291456 | tf_op jit(solution)/shard_map/psum | solution.py:178
  434.6 244.5 %copy-start.27 = (f32[768]{0:T(1024)}, f32[768]{0:T(1024)S(1)}, u32[]{:S(2)}) copy-start(f32[768]{0:T(1024)S(1)} %get-tuple-element.639) | copy-start | bytes 9220
  434.7 370.4 %copy-start.31 = (f32[768]{0:T(1024)}, f32[768]{0:T(1024)S(1)}, u32[]{:S(2)}) copy-start(f32[768]{0:T(1024)S(1)} %get-tuple-element.640) | copy-start | bytes 9220
  465.2 204.5 %copy-start.35 = (f32[768]{0:T(1024)}, f32[768]{0:T(1024)S(1)}, u32[]{:S(2)}) copy-start(f32[768]{0:T(1024)S(1)} %get-tuple-element.637) | copy-start | bytes 9220
  488.0 3.1 copy-start.9
  493.4 3.6 copy-start.29
  575.8 9.3 copy-start.5
  585.0 210.3 %all-reduce.12.cloned.1.call-start = ((), (), s32[]{:S(2)}) async-start(), calls=%async_computation.14 | async-start | bytes 6291456 | tf_op jit(solution)/shard_map/psum | solution.py:194
  674.8 4.4 copy-start.2
  674.8 4.4 copy-start.23
  675.7 3.5 copy-start.6
  675.7 5.7 copy-start.25
  681.4 18.9 copy-start.4
  709.3 713.9 %reduce-scatter.12.cloned.1.call-start = ((), (), s32[]{:S(2)}) async-start(), calls=%async_computation.15 | async-start | bytes 7864320 | tf_op jit(solution)/shard_map/reduce_scatter | solution.py:241
  709.4 95.6 %copy-start.30 = (f32[2048]{0:T(1024)S(1)}, f32[2048]{0:T(1024)}, u32[]{:S(2)}) copy-start(f32[2048]{0:T(1024)} %copy-done.29) | copy-start | bytes 24580
  795.3 9.7 copy-start.11
  805.0 8.9 copy-start.19
  811.3 2.6 copy-start.1
  823.3 6.9 copy-start.13
  823.4 6.9 copy-start.22
  879.9 8.6 copy-start.3
  939.3 9.5 copy-start.3
  999.6 9.5 copy-start.3
  1059.9 9.5 copy-start.3
  1120.2 9.5 copy-start.3
  1180.5 9.5 copy-start.3
  1241.0 9.5 copy-start.3
  1301.4 9.5 copy-start.3
  1312.3 1.9 copy-start
  1312.3 224.4 %reduce-scatter.14.cloned.1.call-start = ((), (), s32[]{:S(2)}) async-start(), calls=%async_computation.16 | async-start | bytes 7864320 | tf_op jit(solution)/shard_map/reduce_scatter | solution.py:244
  1312.9 283.8 %reduce-scatter.22.cloned.1.call-start = ((), (), s32[]{:S(2)}) async-start(), calls=%async_computation.21 | async-start | bytes 417792
  1315.6 339.6 %reduce-scatter.24.cloned.1.call-start = ((), (), s32[]{:S(2)}) async-start(), calls=%async_computation.22 | async-start | bytes 417792
  1321.4 217.9 %copy-start.8 = (bf16[2,1024,768]{2,1,0:T(8,128)(2,1)S(1)}, bf16[2,1024,768]{2,1,0:T(8,128)(2,1)}, u32[]{:S(2)}) copy-start(bf16[2,1024,768]{2,1,0:T(8,128)(2,1)} %param.16) | copy-start | bytes 9437188
  1327.9 448.2 %all-reduce.16.cloned.1.call-start = ((), (), s32[]{:S(2)}) async-start(), calls=%async_computation.23 | async-start | bytes 9437184
  1547.4 6.5 copy-start.20
  1553.8 8.9 copy-start.17
  1553.8 310.0 %all-reduce.14.cloned.1.call-start = ((), (), s32[]{:S(2)}) async-start(), calls=%async_computation.17 | async-start | bytes 6291456 | tf_op jit(solution)/shard_map/psum | solution.py:264
  1562.5 363.6 %reduce-scatter.16.cloned.1.call-start = ((), (), s32[]{:S(2)}) async-start(), calls=%async_computation.18 | async-start | bytes 1253376 | tf_op jit(solution)/shard_map/reduce_scatter | solution.py:272
  1568.4 10.6 copy-start.32
  1568.4 10.6 copy-start.36
  1568.4 436.6 %reduce-scatter.20.cloned.1.call-start = ((), (), s32[]{:S(2)}) async-start(), calls=%async_computation.20 | async-start | bytes 5013504 | tf_op jit(solution)/shard_map/reduce_scatter | solution.py:274
  1579.0 10.7 copy-start.48
  1579.0 11.9 copy-start.24
  1579.0 11.9 copy-start.26
  1579.0 11.9 copy-start.28
  1579.0 11.9 copy-start.34
  1579.0 505.2 %reduce-scatter.18.cloned.1.call-start = ((), (), s32[]{:S(2)}) async-start(), calls=%async_computation.19 | async-start | bytes 5013504 | tf_op jit(solution)/shard_map/reduce_scatter | solution.py:273
  1590.9 65.7 %copy-start.15 = (bf16[2,1024,384]{1,2,0:T(8,128)(2,1)S(1)}, bf16[2,1024,384]{1,2,0:T(8,128)(2,1)}, u32[]{:S(2)}) copy-start(bf16[2,1024,384]{1,2,0:T(8,128)(2,1)} %reduce-scatter.14.cloned.1.call-done) | copy-start | bytes 4718596
  1590.9 66.0 %copy-start.43 = (f32[1536]{0:T(1024)S(1)}, f32[1536]{0:T(1024)}, u32[]{:S(2)}) copy-start(f32[1536]{0:T(1024)} %get-tuple-element.708) | copy-start | bytes 18436
  (9 other events, 9.5 us)
Sparse Core Ops, SparseCore 0:
  10.2 43.1 all-gather.7
  67.8 122.5 all-gather.11
  192.5 113.6 all-gather.9
  404.0 83.9 all-reduce.7
  490.2 42.3 all-gather.13
  534.7 41.0 all-gather.15
  585.1 84.5 all-reduce.9
  709.5 85.8 all-reduce.11
  1312.5 110.7 reduce-scatter.11
  1425.4 111.2 reduce-scatter.13
  1540.2 56.4 reduce-scatter.21
  1600.1 55.0 reduce-scatter.23
  1658.8 117.2 all-reduce.15
  1778.3 85.5 all-reduce.13
  1867.9 58.1 reduce-scatter.15
  1930.4 74.5 reduce-scatter.19
  2009.3 74.8 reduce-scatter.17
where the time goes:
time: 2100 us; the launch traced here: 2090 us
  waiting for transfers between devices  977 us (47%)
  matrix products  697 us (33%)
  blocking collectives  174 us (8%)
  local copies, waits for them, and re-layouts  134 us (6%)
  other arithmetic  92 us (4%)
    dot_general x16, matrix products, block_scores(): jnp.einsum('sqhd,skhd->shqk', query_four, key_four, preferred_element_typ...  141 us
    unnamed x20, waiting for transfers between devices  119 us
    dot_general x8, matrix products, score_grads(): jnp.einsum('sqhd,skhd->shqk', grad_four, value_four, preferred_element_ty...  116 us
    reduce_scatter x1, waiting for transfers between devices, body(): lax.psum_scatter(value_all.astype(jnp.bfloat16), 'ctx', scatter_dimension...  111 us
    reduce_scatter x1, waiting for transfers between devices, body(): lax.psum_scatter(key_all.astype(jnp.bfloat16), 'ctx', scatter_dimension=1...  95.3 us
    dot_general x8, matrix products, grad_step(): jnp.einsum('shqk,sqhd->skhd', prob_low, grad_four, preferred_element_type...  89.2 us
    psum x1, waiting for transfers between devices, body(): lax.psum(input_part.astype(jnp.bfloat16), 'tp').astype(jnp.float32)  86.1 us
    psum x1, waiting for transfers between devices, body(): lax.psum(back_part.astype(jnp.bfloat16), 'tp').astype(jnp.float32)  85.9 us
  transfers between devices with their start and end apart: 17, of which 17 were waited for; matrix products, arithmetic and copies ran while one was open for 12% of the time, Pallas kernels for 0%

commit v1 on v0

--- a/solution.py
+++ b/solution.py
@@ -7,6 +7,20 @@
 epsilon = 1e-12
 score_scale = 0.125
 highest = lax.Precision.HIGHEST
+
+
+def produce_rails(row_data):
+    local_out, seen_now = (lax.axis_size(("fsdp", "ctx")), lax.axis_index(("fsdp", "ctx")))
+    piece_next, v_next = (row_data, 1)
+    while v_next < local_out:
+        w_next = lax.ppermute(
+            piece_next, ("fsdp", "ctx"), list(map(lambda k0: (k0, k0 ^ v_next), range(local_out)))
+        )
+        near = jnp.concatenate([piece_next, w_next], axis=0)
+        block_now = jnp.concatenate([w_next, piece_next], axis=0)
+        piece_next = jnp.where(seen_now & v_next == 0, near, block_now)
+        v_next = 2 * v_next
+    return piece_next
 
 
 def contract_last(left, right):
@@ -91,7 +105,7 @@
         return array_two.reshape(seq_count, array_two.shape[0] // seq_count, array_two.shape[1])
 
     gathered = (
-        lax.all_gather(qkv_weight, ("fsdp", "ctx"), axis=0, tiled=True),
+        produce_rails(qkv_weight),
         lax.all_gather(out_weight, ("fsdp", "ctx"), axis=0, tiled=True),
         lax.all_gather(up_weight, ("fsdp", "ctx"), axis=0, tiled=True),
         lax.all_gather(down_weight, ("fsdp", "ctx"), axis=0, tiled=True),

time: 2100 us -> 1950 us (0.929)
  waiting for transfers between devices: 977 us -> 704 us
  other arithmetic: 92 us -> 154 us
  matrix products: 697 us -> 727 us
    reduce_scatter x1, waiting for transfers between devices: 56.6 us -> 0.01 us  [body(): lax.psum_scatter(out_grad, ('fsdp', 'ctx'), scatter_dimension=0, tiled=True)]
    psum x1, waiting for transfers between devices: 86.1 us -> 31.7 us  [body(): lax.psum(input_part.astype(jnp.bfloat16), 'tp').astype(jnp.float32)]
    reduce_sum x8, other arithmetic: 34.4 us -> 83.8 us  [stats_step(): jnp.sum(jnp.exp(scores - new_max[..., None]), axis=-1)]
    unnamed x20 -> x19, waiting for transfers between devices: 119 us -> 69.5 us
    all_gather x1 -> x0, waiting for transfers between devices: 45.5 us -> none  [body(): lax.all_gather(qkv_weight, ('fsdp', 'ctx'), axis=0, tiled=True)]
    dot_general x16, matrix products: 141 us -> 181 us  [block_scores(): jnp.einsum('sqhd,skhd->shqk', query_four, key_four, preferred_element_typ...]
    reduce_scatter x1, waiting for transfers between devices: 78.9 us -> 40.1 us  [body(): lax.psum_scatter(down_grad, ('fsdp', 'ctx'), scatter_dimension=0, tiled=T...]
    ppermute x0 -> x4, waiting for transfers between devices: none -> 35.7 us  [produce_rails(): lax.ppermute(piece_next, ('fsdp', 'ctx'), list(map(lambda k0: (k0, k0 ^ v...]
  transfers between devices with their start and end apart: 17 -> 20, of which waited for: 17 -> 15; matrix products, arithmetic and copies ran while one was open for 12% -> 18% of each run, Pallas kernels for 0% -> 0%
where the time goes in v1:
time: 1950 us; the launch traced here: 1940 us
  matrix products  727 us (37%)
  waiting for transfers between devices  704 us (36%)
  blocking collectives  176 us (9%)
  other arithmetic  154 us (8%)
  local copies, waits for them, and re-layouts  150 us (8%)
    dot_general x16, matrix products, block_scores(): jnp.einsum('sqhd,skhd->shqk', query_four, key_four, preferred_element_typ...  181 us
    dot_general x8, matrix products, score_grads(): jnp.einsum('sqhd,skhd->shqk', grad_four, value_four, preferred_element_ty...  116 us
    reduce_scatter x1, waiting for transfers between devices, body(): lax.psum_scatter(value_all.astype(jnp.bfloat16), 'ctx', scatter_dimension...  111 us
    reduce_scatter x1, waiting for transfers between devices, body(): lax.psum_scatter(key_all.astype(jnp.bfloat16), 'ctx', scatter_dimension=1...  95.2 us
    psum x1, waiting for transfers between devices, body(): lax.psum(back_part.astype(jnp.bfloat16), 'tp').astype(jnp.float32)  85.7 us
    reduce_sum x8, other arithmetic, stats_step(): jnp.sum(jnp.exp(scores - new_max[..., None]), axis=-1)  83.8 us
    psum x1, waiting for transfers between devices, body(): lax.psum(ffn_part.astype(jnp.bfloat16), 'tp').astype(jnp.float32)  83.5 us
    dot_general x8, matrix products, grad_step(): jnp.einsum('shqk,sqhd->skhd', prob_low, grad_four, preferred_element_type...  82.4 us
  transfers between devices with their start and end apart: 20, of which 15 were waited for; matrix products, arithmetic and copies ran while one was open for 18% of the time, Pallas kernels for 0%

profile of v1, /device:TPU:0, one launch (start us, length us, event | category | flops | bytes accessed | tf_op | source)
XLA Modules:
  0.0 1939.0 jit_solution(15432669599757194950)
XLA Ops:
  23.1 13.0 collective-permute-done.1
  56.8 13.6 collective-permute-done.3
  84.2 55.4 %all_gather.23 = bf16[768,384]{1,0:T(8,128)(2,1)} all-gather(bf16[48,384]{1,0:T(8,128)(2,1)S(1)} %copy-done.35), channel_id=1, replica_groups=mesh['fsdp'=4,'ctx'=4,'tp'=2] {'fsdp','ctx'}, dimensions={0}, use_global_device_ids=true | all-gather | bytes 626688 | tf_op jit(solution)/shard_map/all_gather | solution.py:109
  158.9 49.4 %all-gather.9.cloned.1.call-done = bf16[2,4096,384]{2,1,0:T(8,128)(2,1)} async-done(((bf16[2,1024,384]{2,1,0:T(8,128)(2,1)}), bf16[2,4096,384]{2,1,0:T(8,128)(2,1)}) %all-gather.9.cloned.1.call-update) | async-done | bytes 6291472 | tf_op jit(solution)/shard_map/all_gather | solution.py:130
  217.2 175.3 %while.48 = (s32[]{:T(128)}, f32[2,6,1024]{2,1,0:T(8,128)S(1)}, f32[2,6,1024]{2,1,0:T(8,128)S(1)}, bf16[2,4096,384]{1,2,0:T(8,128)(2,1)}, bf16[2,1024,6,64]{1,3,...) while((s32[]{:T(128)}, f32[2,6,1024]{2,1,0:T(8,128)S(1)}, ...), condition=%wide.region_3.4_spmd.clone, body=%wide.region_0.3_spmd.clone.sunk | while | flops 836825088 | bytes 54902936 | solution.py:155
  218.5 10.2 bitcast_reduce_fusion.2
  228.6 10.5 fusion.102
  240.4 10.2 bitcast_reduce_fusion.2
  250.6 10.6 fusion.102
  262.5 10.2 bitcast_reduce_fusion.2
  272.7 10.5 fusion.102
  284.5 10.2 bitcast_reduce_fusion.2
  294.7 10.4 fusion.102
  306.4 10.1 bitcast_reduce_fusion.2
  316.5 10.4 fusion.102
  328.2 10.1 bitcast_reduce_fusion.2
  338.3 10.4 fusion.102
  350.1 10.1 bitcast_reduce_fusion.2
  360.2 10.4 fusion.102
  371.9 10.1 bitcast_reduce_fusion.2
  382.0 10.4 fusion.102
  401.3 85.8 %while.49 = (s32[]{:T(128)}, f32[2,1024,6,64]{1,3,2,0:T(8,128)}, bf16[2,4096,384]{1,2,0:T(8,128)(2,1)}, bf16[2,4096,384]{1,2,0:T(8,128)(2,1)}, bf16[2,1024,6,64]...) while((s32[]{:T(128)}, f32[2,1024,6,64]{1,3,2,0:T(8,128)}, ...), condition=%wide.region_5.6_spmd.clone, body=%wide.region_4.5_spmd.clone.sunk | while | flops 1637351424 | bytes 12681385 | solution.py:178
  466.7 9.4 bitcast_add_fusion.4
  497.9 30.4 %all-gather = bf16[16,48,4]{1,2,0:T(4,128)(2,1)S(1)} all-gather(bf16[1,48,4]{1,2,0:T(4,128)(2,1)S(1)} %bitcast.198), channel_id=1, replica_groups=mesh['fsdp'=4,'ctx'=4,'tp'=2] {'fsdp','ctx'}, dimensions={0}, use_global_device_ids=true | all-gather | bytes 6528 | tf_op jit(solution)/shard_map/all_gather | solution.py:113
  529.0 29.2 %all-gather.1 = bf16[16,48,2]{1,2,0:T(2,128)(2,1)S(1)} all-gather(bf16[1,48,2]{1,2,0:T(2,128)(2,1)S(1)} %bitcast.199), channel_id=1, replica_groups=mesh['fsdp'=4,'ctx'=4,'tp'=2] {'fsdp','ctx'}, dimensions={0}, use_global_device_ids=true | all-gather | bytes 3264 | tf_op jit(solution)/shard_map/all_gather | solution.py:112
  558.4 23.3 %all-reduce.8.cloned.1.call-done = bf16[2048,768]{1,0:T(8,128)(2,1)} async-done(((bf16[2048,768]{1,0:T(8,128)(2,1)}), bf16[2048,768]{1,0:T(8,128)(2,1)}) %all-reduce.8.cloned.1.call-update) | async-done | bytes 3145744 | tf_op jit(solution)/shard_map/psum | solution.py:181
  591.9 35.1 %multiply_convert_fusion.1 = (bf16[2048,1536]{1,0:T(8,128)(2,1)}, f32[2048,1536]{1,0:T(8,128)}, f32[2048,1536]{1,0:T(8,128)}) fusion(f32[1536]{0:T(1024)S(1)} %convert_element_type.186, bf16[768,1536]{1,0:T(8,128)(2,1)} %all-gather.11.cloned.1.call-done, f32[2048,768]{1,0:T(8,128)} %subtract_multiply_fusion.2, f32[768]{0:T(1024)S(1)} %get-tuple-element.637, ...), kind=kOutput, calls=%fused_computation.29 | convolution fusion | flops 5044174848 | bytes 40120320 | tf_op jit(solution)/shard_map/dot_general | solution.py:186
  638.7 83.5 %all-reduce.10.cloned.1.call-done = bf16[2048,768]{1,0:T(8,128)(2,1)} async-done(((bf16[2048,768]{1,0:T(8,128)(2,1)}), bf16[2048,768]{1,0:T(8,128)(2,1)}) %all-reduce.10.cloned.1.call-update) | async-done | bytes 3145744 | tf_op jit(solution)/shard_map/psum | solution.py:192
  733.6 18.8 convert_reduce_fusion
  761.8 85.7 %all-reduce.12.cloned.1.call-done = bf16[2048,768]{1,0:T(8,128)(2,1)} async-done(((bf16[2048,768]{1,0:T(8,128)(2,1)}), bf16[2048,768]{1,0:T(8,128)(2,1)}) %all-reduce.12.cloned.1.call-update) | async-done | bytes 3145744 | tf_op jit(solution)/shard_map/psum | solution.py:208
  882.1 474.3 %while.50 = (s32[]{:T(128)}, f32[2,1024,6,64]{1,3,2,0:T(8,128)}, bf16[2,4096,384]{1,2,0:T(8,128)(2,1)}, bf16[2,4096,384]{1,2,0:T(8,128)(2,1)}, bf16[2,4096,384]{...) while((s32[]{:T(128)}, f32[2,1024,6,64]{1,3,2,0:T(8,128)}, ...), condition=%wide.region_18.19_spmd.clone, body=%wide.region_17.18_spmd.clone.sunk | while | flops 4072931328 | bytes 136200400 | solution.py:251
  883.5 12.5 exponential_divide_fusion.2
  897.2 14.5 multiply_convert_fusion.5
  920.7 10.3 fusion.117
  941.9 12.5 exponential_divide_fusion.2
  955.6 14.5 multiply_convert_fusion.5
  979.1 10.3 fusion.117
  1001.3 12.5 exponential_divide_fusion.2
  1015.0 14.5 multiply_convert_fusion.5
  1038.4 10.3 fusion.117
  1060.7 12.5 exponential_divide_fusion.2
  1074.4 14.5 multiply_convert_fusion.5
  1097.8 10.3 fusion.117
  1120.2 12.5 exponential_divide_fusion.2
  1133.9 14.5 multiply_convert_fusion.5
  1157.3 10.3 fusion.117
  1179.6 12.5 exponential_divide_fusion.2
  1193.3 14.5 multiply_convert_fusion.5
  1216.7 10.3 fusion.117
  1239.0 12.5 exponential_divide_fusion.2
  1252.7 14.5 multiply_convert_fusion.5
  1276.1 10.3 fusion.117
  1298.3 12.5 exponential_divide_fusion.2
  1312.0 14.5 multiply_convert_fusion.5
  1335.4 10.3 fusion.117
  1372.3 95.2 %reduce-scatter.12.cloned.1.call-done = bf16[2,1024,384]{1,2,0:T(8,128)(2,1)} async-done(((bf16[2,4096,384]{1,2,0:T(8,128)(2,1)}), bf16[2,1024,384]{1,2,0:T(8,128)(2,1)}) %reduce-scatter.12.cloned.1.call-update) | async-done | bytes 1572880 | tf_op jit(solution)/shard_map/reduce_scatter | solution.py:255
  1470.1 111.0 %reduce-scatter.14.cloned.1.call-done = bf16[2,1024,384]{1,2,0:T(8,128)(2,1)} async-done(((bf16[2,4096,384]{1,2,0:T(8,128)(2,1)}), bf16[2,1024,384]{1,2,0:T(8,128)(2,1)}) %reduce-scatter.14.cloned.1.call-update) | async-done | bytes 1572880 | tf_op jit(solution)/shard_map/reduce_scatter | solution.py:258
  1613.6 10.6 fusion.47
  1624.3 10.6 fusion.37
  1647.5 62.6 %reduce-scatter.24.cloned.1.call-done = f32[48,4]{1,0:T(8,128)} async-done(((f32[768,4]{1,0:T(8,128)}), f32[48,4]{1,0:T(8,128)}) %reduce-scatter.24.cloned.1.call-update) | async-done | bytes 784
  1711.8 61.1 %all-reduce.1 = (f32[2,384]{1,0:T(2,128)}, f32[1536]{0:T(1024)}) all-reduce(f32[2,384]{1,0:T(2,128)S(1)} %pad_maximum_fusion.5, f32[1536]{0:T(1024)S(1)} %copy-done.45), channel_id=1, replica_groups=mesh['fsdp'=4,'ctx'=4,'tp'=2] {'fsdp','ctx'}, use_global_device_ids=true, to_apply=%region_25.26 | all-reduce | flops 2304 | bytes 18432 | tf_op jit(solution)/shard_map/psum | solution.py:292
  1774.6 31.7 %all-reduce.14.cloned.1.call-done = bf16[2048,768]{1,0:T(8,128)(2,1)} async-done(((bf16[2048,768]{1,0:T(8,128)(2,1)}), bf16[2048,768]{1,0:T(8,128)(2,1)}) %all-reduce.14.cloned.1.call-update) | async-done | bytes 3145744 | tf_op jit(solution)/shard_map/psum | solution.py:278
  1812.0 40.1 %reduce-scatter.20.cloned.1.call-done = f32[48,1536]{1,0:T(8,128)} async-done(((f32[768,1536]{1,0:T(8,128)}), f32[48,1536]{1,0:T(8,128)}) %reduce-scatter.20.cloned.1.call-update) | async-done | bytes 294928 | tf_op jit(solution)/shard_map/reduce_scatter | solution.py:288
  1852.1 79.1 %reduce-scatter.18.cloned.1.call-done = f32[48,1536]{1,0:T(8,128)} async-done(((f32[768,1536]{1,0:T(8,128)}), f32[48,1536]{1,0:T(8,128)}) %reduce-scatter.18.cloned.1.call-update) | async-done | bytes 294928 | tf_op jit(solution)/shard_map/reduce_scatter | solution.py:287
  (337 shorter events, 508.4 us)
Async XLA Ops:
  8.0 41.8 %copy-start.24 = (bf16[48,3,384]{2,0,1:T(8,128)(2,1)S(1)}, bf16[48,3,384]{2,0,1:T(8,128)(2,1)}, u32[]{:S(2)}) copy-start(bf16[48,3,384]{2,0,1:T(8,128)(2,1)} %param.17) | copy-start | bytes 331780
  8.0 200.3 %all-gather.9.cloned.1.call-start = ((), (), s32[]{:S(2)}) async-start(), calls=%async_computation.8 | async-start | bytes 7864320 | tf_op jit(solution)/shard_map/all_gather | solution.py:130
  9.2 10.1 collective-permute-start
  20.4 52.2 %copy-start.7 = (bf16[2,1024,768]{2,1,0:T(8,128)(2,1)S(1)}, bf16[2,1024,768]{2,1,0:T(8,128)(2,1)}, u32[]{:S(2)}) copy-start(bf16[2,1024,768]{2,1,0:T(8,128)(2,1)} %param.16) | copy-start | bytes 9437188
  20.4 15.7 collective-permute-start.1
  40.8 2.1 collective-permute-start.2
  48.4 22.0 %collective-permute-start.3 = (bf16[384,3,384]{0,2,1:T(8,128)(2,1)}, bf16[384,3,384]{0,2,1:T(8,128)(2,1)}, u32[]{:S(2)}, u32[]{:S(2)}) collective-permute-start(bf16[384,3,384]{0,2,1:T(8,128)(2,1)} %maximum_select_fusion.5), channel_id=1, source_target_pairs={{0,16},{2,18},{4,20},{6,22},{8,24},{10,26},{12,28},{14,30},{16,0},... | collective-permute-start | bytes 2654216 | tf_op jit(solution)/shard_map/ppermute | solution.py:16
  78.6 3.6 copy-start.15
  78.6 5.5 copy-start.47
  78.6 5.6 copy-start.35
  84.0 308.5 %all-gather.7.cloned.1.call-start = ((), (), s32[]{:S(2)}) async-start(), calls=%async_computation.7 | async-start | bytes 7864320 | tf_op jit(solution)/shard_map/all_gather | solution.py:133
  158.9 422.8 %all-reduce.8.cloned.1.call-start = ((), (), s32[]{:S(2)}) async-start(), calls=%async_computation.9 | async-start | bytes 6291456 | tf_op jit(solution)/shard_map/psum | solution.py:181
  487.0 9.6 copy-start.4
  487.1 9.6 copy-start.13
  487.1 9.6 copy-start.21
  487.1 6.0 copy-start.19
  491.9 1.2 copy-start.17
  493.1 4.8 copy-start.48
  493.1 35.9 %copy-start.49 = (bf16[48,2]{0,1:T(2,128)(2,1)S(1)}, bf16[48,2]{0,1:T(2,128)(2,1)}, u32[]{:S(2)}) copy-start(bf16[48,2]{0,1:T(2,128)(2,1)} %param.23) | copy-start | bytes 580
  493.1 65.3 %copy-start.46 = (bf16[1536]{0:T(1024)(128)(2,1)S(1)}, bf16[1536]{0:T(1024)(128)(2,1)}, u32[]{:S(2)}) copy-start(bf16[1536]{0:T(1024)(128)(2,1)} %param.21) | copy-start | bytes 9220
  496.6 89.2 %copy-start.8 = (bf16[2,1024,768]{2,1,0:T(8,128)(2,1)S(1)}, bf16[2,1024,768]{2,1,0:T(8,128)(2,1)}, u32[]{:S(2)}) copy-start(bf16[2,1024,768]{2,1,0:T(8,128)(2,1)} %param.16) | copy-start | bytes 9437188
  496.7 95.3 %all-gather.11.cloned.1.call-start = ((), (), s32[]{:S(2)}) async-start(), calls=%async_computation.10 | async-start | bytes 2506752 | tf_op jit(solution)/shard_map/all_gather | solution.py:110
  497.3 129.8 %all-gather.13.cloned.1.call-start = ((), (), s32[]{:S(2)}) async-start(), calls=%async_computation.11 | async-start | bytes 2506752 | tf_op jit(solution)/shard_map/all_gather | solution.py:111
  497.8 224.4 %all-reduce.10.cloned.1.call-start = ((), (), s32[]{:S(2)}) async-start(), calls=%async_computation.12 | async-start | bytes 6291456 | tf_op jit(solution)/shard_map/psum | solution.py:192
  529.0 193.3 %copy-start.37 = (f32[768]{0:T(1024)}, f32[768]{0:T(1024)S(1)}, u32[]{:S(2)}) copy-start(f32[768]{0:T(1024)S(1)} %get-tuple-element.637) | copy-start | bytes 9220
  558.4 173.0 %copy-start.29 = (f32[768]{0:T(1024)}, f32[768]{0:T(1024)S(1)}, u32[]{:S(2)}) copy-start(f32[768]{0:T(1024)S(1)} %get-tuple-element.639) | copy-start | bytes 9220
  558.4 298.5 %copy-start.33 = (f32[768]{0:T(1024)}, f32[768]{0:T(1024)S(1)}, u32[]{:S(2)}) copy-start(f32[768]{0:T(1024)S(1)} %get-tuple-element.640) | copy-start | bytes 9220
  581.7 4.1 copy-start.10
  627.1 9.7 copy-start.5
  636.3 211.2 %all-reduce.12.cloned.1.call-start = ((), (), s32[]{:S(2)}) async-start(), calls=%async_computation.13 | async-start | bytes 6291456 | tf_op jit(solution)/shard_map/psum | solution.py:208
  727.3 4.0 copy-start.2
  727.4 4.0 copy-start.25
  728.2 3.2 copy-start.6
  728.3 5.4 copy-start.27
  733.6 18.8 copy-start.3
  761.5 706.0 %reduce-scatter.12.cloned.1.call-start = ((), (), s32[]{:S(2)}) async-start(), calls=%async_computation.14 | async-start | bytes 7864320 | tf_op jit(solution)/shard_map/reduce_scatter | solution.py:255
  761.8 95.1 %copy-start.32 = (f32[2048]{0:T(1024)S(1)}, f32[2048]{0:T(1024)}, u32[]{:S(2)}) copy-start(f32[2048]{0:T(1024)} %copy-done.31) | copy-start | bytes 24580
  847.5 9.4 copy-start.12
  856.9 8.9 copy-start.20
  863.2 2.6 copy-start.1
  872.1 1.9 copy-start.11
  875.3 6.9 copy-start.14
  875.3 6.9 copy-start.22
  1356.5 2.0 copy-start
  1356.5 224.6 %reduce-scatter.14.cloned.1.call-start = ((), (), s32[]{:S(2)}) async-start(), calls=%async_computation.15 | async-start | bytes 7864320 | tf_op jit(solution)/shard_map/reduce_scatter | solution.py:258
  1357.3 288.9 %reduce-scatter.22.cloned.1.call-start = ((), (), s32[]{:S(2)}) async-start(), calls=%async_computation.20 | async-start | bytes 417792
  1359.9 350.2 %reduce-scatter.24.cloned.1.call-start = ((), (), s32[]{:S(2)}) async-start(), calls=%async_computation.21 | async-start | bytes 417792
  1365.7 218.0 %copy-start.9 = (bf16[2,1024,768]{2,1,0:T(8,128)(2,1)S(1)}, bf16[2,1024,768]{2,1,0:T(8,128)(2,1)}, u32[]{:S(2)}) copy-start(bf16[2,1024,768]{2,1,0:T(8,128)(2,1)} %param.16) | copy-start | bytes 9437188
  1372.3 400.6 %all-reduce.16.cloned.1.call-start = ((), (), s32[]{:S(2)}) async-start(), calls=%async_computation.22 | async-start | bytes 9437184
  1591.8 6.5 copy-start.23
  1598.2 9.5 copy-start.18
  1598.3 208.1 %all-reduce.14.cloned.1.call-start = ((), (), s32[]{:S(2)}) async-start(), calls=%async_computation.16 | async-start | bytes 6291456 | tf_op jit(solution)/shard_map/psum | solution.py:278
  1607.5 204.4 %reduce-scatter.16.cloned.1.call-start = ((), (), s32[]{:S(2)}) async-start(), calls=%async_computation.17 | async-start | bytes 1253376 | tf_op jit(solution)/shard_map/reduce_scatter | solution.py:286
  1613.5 10.8 copy-start.34
  1613.5 10.8 copy-start.38
  1613.5 238.6 %reduce-scatter.20.cloned.1.call-start = ((), (), s32[]{:S(2)}) async-start(), calls=%async_computation.19 | async-start | bytes 5013504 | tf_op jit(solution)/shard_map/reduce_scatter | solution.py:288
  1624.1 10.8 copy-start.50
  1624.2 12.0 copy-start.26
  1624.2 12.0 copy-start.28
  1624.2 12.0 copy-start.30
  1624.2 12.0 copy-start.36
  1624.2 307.0 %reduce-scatter.18.cloned.1.call-start = ((), (), s32[]{:S(2)}) async-start(), calls=%async_computation.18 | async-start | bytes 5013504 | tf_op jit(solution)/shard_map/reduce_scatter | solution.py:287
  1636.2 75.2 %copy-start.16 = (bf16[2,1024,384]{1,2,0:T(8,128)(2,1)S(1)}, bf16[2,1024,384]{1,2,0:T(8,128)(2,1)}, u32[]{:S(2)}) copy-start(bf16[2,1024,384]{1,2,0:T(8,128)(2,1)} %reduce-scatter.14.cloned.1.call-done) | copy-start | bytes 4718596
  1636.2 75.5 %copy-start.45 = (f32[1536]{0:T(1024)S(1)}, f32[1536]{0:T(1024)}, u32[]{:S(2)}) copy-start(f32[1536]{0:T(1024)} %get-tuple-element.708) | copy-start | bytes 18436
  (7 other events, 6.1 us)
Sparse Core Ops, SparseCore 0:
  84.1 124.1 all-gather.8
  210.5 114.2 all-gather.6
  496.8 84.8 all-reduce.7
  636.4 85.7 all-reduce.9
  761.6 85.8 all-reduce.11
  1356.7 110.7 reduce-scatter.11
  1469.8 111.2 reduce-scatter.13
  1584.6 61.5 reduce-scatter.21
  1649.7 60.3 reduce-scatter.23
  1714.1 58.8 reduce-scatter.15
  1777.5 74.5 reduce-scatter.19
  1856.4 74.7 reduce-scatter.17
Sparse Core Ops, SparseCore 1:
  499.5 41.4 all-gather.10
  543.1 40.7 all-gather.12
  1598.3 120.1 all-reduce.15
  1720.8 85.4 all-reduce.13
